TPU v7x, 256 devices: a whole 4x4x8 slice. The times are simulated.
256 devices in a mesh: req: 32 (over y, z), head: 8 (over x, core).
Axes of the slice: x: 4, y: 4, z: 8, core: 2. Of those that a mesh axis runs over, the one named last changes fastest.
Arguments:
- tokens: bfloat16 [256, 1024], P('req'), may hold values from -6 to 6
- lengths: int32 [256], P('req'), may hold values from 1 to 512, as said below
- slot_owner: int32 [256], P('req'), may hold values from 0 to 255, as said below
- positions: int32 [256], P('req'), may hold values from 0 to 8191
- variates: int32 [256], P('req'), may hold values from 0 to 7
- cache_variates: int32 [256, 512], P('req'), may hold values from 0 to 7
- kv_cache: bfloat16 [2, 2, 256, 512, 1024], P(None, None, 'req', None, 'head'), may hold values from -6 to 6
- attn_gain: float32 [2, 1024], replicated, may hold values from 0.1 to 1.9
- ffn_gain: float32 [2, 1024], replicated, may hold values from 0.1 to 1.9
- qkv_weight: bfloat16 [2, 1024, 3072], P(None, None, 'head'), may hold values from -0.1875 to 0.1875
- out_weight: bfloat16 [2, 1024, 1024], P(None, 'head'), may hold values from -0.1875 to 0.1875
- gate_up_weight: bfloat16 [2, 2, 1024, 4096], P(None, None, None, 'head'), may hold values from -0.1875 to 0.1875
- down_weight: bfloat16 [2, 4096, 1024], P(None, 'head'), may hold values from -0.09375 to 0.09375
- variate_bias: float32 [2, 2, 16], P(None, None, 'head'), may hold values from -2 to 300
Outputs:
- next_states: bfloat16 [256, 1024], P(('req', 'head'))
Inputs may be any that keep to these rules, and one draw needn't show every extreme that they name: `lengths`: live cache positions of each request; the largest is exactly 512 in every draw. `slot_owner`: each request is held in exactly one slot; taken in an order of non-increasing length, the requests fill slot t of every req index in turn t = 0, 1, ..., the req indices in rising order on even turns and in falling order on odd ones; no two slots of one req index hold requests of the same device of next_states (the same 1 request).
All inputs are finite; a program needn't handle non-finite values.
Results may differ from a plain program's by a relative error of at most 0.02.
Values may be sent and summed in bfloat16 or wider, within the bound.
A program may use at most 64 MiB of HBM per device.

v0:
```python
import jax
import jax.numpy as jnp
from jax import lax
from jax.sharding import PartitionSpec as P

HD = 64
LAYERS = 2


neg_fill = -1e30


def rms_scale(stream, gain_row):
    return stream * lax.rsqrt(jnp.mean(stream * stream, axis=-1, keepdims=True) + 1e-06) * gain_row


def rotary(vectors, time_ids):
    half_width = vectors.shape[-1] // 2
    frequency = 10000.0 ** (-2.0 * jnp.arange(half_width, dtype=jnp.float32) / vectors.shape[-1])
    angles = time_ids.astype(jnp.float32)[:, None, None] * frequency[None, None, :]
    cosine = jnp.cos(angles)
    sine_part = jnp.sin(angles)
    front_half = vectors[..., :half_width]
    back_half = vectors[..., half_width:]
    return jnp.concatenate(
        [front_half * cosine - back_half * sine_part, front_half * sine_part + back_half * cosine],
        axis=-1,
    )


def attend(
    queries,
    key_new,
    value_new,
    cached_keys,
    cached_values,
    cache_var,
    cache_lengths,
    variate_ids,
    same_bias,
    diff_bias,
):
    row_count, cache_len, width = cached_keys.shape
    local_heads = queries.shape[1]
    score_scale = HD ** (-0.5)
    diagonal_mask = jnp.eye(local_heads, dtype=jnp.bfloat16)
    q_block = (queries[:, :, :, None] * diagonal_mask[None, :, None, :]).reshape(
        row_count, local_heads * HD, local_heads
    )
    raw_scores = jnp.einsum(
        "rcf,rfh->rch", cached_keys, q_block, preferred_element_type=jnp.float32
    )
    score_bias = jnp.where(
        (cache_var == variate_ids[:, None])[:, :, None],
        same_bias[None, None, :],
        diff_bias[None, None, :],
    )
    scores = raw_scores * score_scale + score_bias
    live_mask = jnp.arange(cache_len, dtype=jnp.int32)[None, :] < cache_lengths[:, None]
    scores = jnp.where(live_mask[:, :, None], scores, neg_fill)
    self_score = (
        jnp.sum(queries.astype(jnp.float32) * key_new.astype(jnp.float32), axis=-1) * score_scale
        + same_bias[None, :]
    )
    row_top = jnp.maximum(jnp.max(scores, axis=1), self_score)
    weights = jnp.exp(scores - row_top[:, None, :])
    self_weight = jnp.exp(self_score - row_top)
    denominator = jnp.sum(weights, axis=1) + self_weight
    probs_bf16 = (weights / denominator[:, None, :]).astype(jnp.bfloat16)
    self_prob = (self_weight / denominator).astype(jnp.bfloat16)
    mixed_full = jnp.einsum(
        "rch,rcf->rhf", probs_bf16, cached_values, preferred_element_type=jnp.float32
    )
    mask_float = diagonal_mask.astype(jnp.float32)
    mixed_heads = jnp.sum(
        mixed_full.reshape(row_count, local_heads, local_heads, HD) * mask_float[None, :, :, None],
        axis=2,
    )
    mixed_heads = mixed_heads + self_prob.astype(jnp.float32)[:, :, None] * value_new.astype(
        jnp.float32
    )
    return mixed_heads.reshape(row_count, local_heads * HD).astype(jnp.bfloat16)


def per_device(
    tokens,
    lengths,
    slot_owner,
    positions,
    variates,
    cache_variates,
    kv_cache,
    attn_gain,
    ffn_gain,
    qkv_weight,
    out_weight,
    gate_up_weight,
    down_weight,
    variate_bias,
):
    head_count = lax.axis_size("head")
    head_place = lax.axis_index("head")
    slot_count = slot_owner.shape[0]
    token_share = slot_count // head_count
    all_lengths, all_times, all_variates, all_owners = (
        lax.all_gather(lengths, "req", axis=0, tiled=True),
        lax.all_gather(positions, "req", axis=0, tiled=True),
        lax.all_gather(variates, "req", axis=0, tiled=True),
        lax.all_gather(slot_owner, "req", axis=0, tiled=True),
    )
    all_tokens = lax.all_gather(tokens, "req", axis=0, tiled=True)
    slot_tokens = jnp.take(all_tokens, slot_owner, axis=0).astype(jnp.float32)
    cache_lengths = jnp.take(all_lengths, slot_owner)
    time_ids = jnp.take(all_times, slot_owner)
    variate_ids = jnp.take(all_variates, slot_owner)
    residual = lax.dynamic_slice_in_dim(slot_tokens, head_place * token_share, token_share, 0)
    local_heads = kv_cache.shape[-1] // HD
    for layer_index in range(LAYERS):
        if layer_index == 0:
            normed = rms_scale(slot_tokens, attn_gain[0]).astype(jnp.bfloat16)
        else:
            normed = lax.all_gather(
                rms_scale(residual, attn_gain[layer_index]).astype(jnp.bfloat16),
                "head",
                axis=0,
                tiled=True,
            )
        projected = jnp.dot(normed, qkv_weight[layer_index], preferred_element_type=jnp.float32)
        projected = projected.reshape(slot_count, local_heads, 3, HD)
        queries = rotary(projected[:, :, 0], time_ids).astype(jnp.bfloat16)
        key_new = rotary(projected[:, :, 1], time_ids).astype(jnp.bfloat16)
        value_new = projected[:, :, 2].astype(jnp.bfloat16)
        attended = attend(
            queries,
            key_new,
            value_new,
            kv_cache[layer_index, 0],
            kv_cache[layer_index, 1],
            cache_variates,
            cache_lengths,
            variate_ids,
            variate_bias[layer_index, 0],
            variate_bias[layer_index, 1],
        )
        out_partial = jnp.dot(attended, out_weight[layer_index], preferred_element_type=jnp.float32)
        residual = residual + lax.psum_scatter(
            out_partial.astype(jnp.bfloat16), "head", scatter_dimension=0, tiled=True
        ).astype(jnp.float32)
        ffn_input = lax.all_gather(
            rms_scale(residual, ffn_gain[layer_index]).astype(jnp.bfloat16),
            "head",
            axis=0,
            tiled=True,
        )
        paired = jnp.einsum(
            "rd,gdf->grf",
            ffn_input,
            gate_up_weight[layer_index],
            preferred_element_type=jnp.float32,
        )
        hidden = (jax.nn.silu(paired[0]) * paired[1]).astype(jnp.bfloat16)
        ffn_partial = jnp.dot(hidden, down_weight[layer_index], preferred_element_type=jnp.float32)
        residual = residual + lax.psum_scatter(
            ffn_partial.astype(jnp.bfloat16), "head", scatter_dimension=0, tiled=True
        ).astype(jnp.float32)
    final_rows = residual.astype(jnp.bfloat16)
    own_place = lax.axis_index("req") * head_count + head_place
    request_ids = own_place * token_share + jnp.arange(token_share, dtype=jnp.int32)
    matches = all_owners[None, :] == request_ids[:, None]
    slot_index = jnp.sum(
        jnp.where(matches, jnp.arange(all_owners.shape[0], dtype=jnp.int32)[None, :], 0), axis=1
    )
    everything = lax.all_gather(final_rows, ("req", "head"), axis=0, tiled=True)
    return jnp.take(everything, slot_index, axis=0)


def solution(mesh):
    return jax.shard_map(
        per_device,
        mesh=mesh,
        in_specs=(
            P("req", None),
            P("req"),
            P("req"),
            P("req"),
            P("req"),
            P("req", None),
            P(None, None, "req", None, "head"),
            P(),
            P(),
            P(None, None, "head"),
            P(None, "head", None),
            P(None, None, None, "head"),
            P(None, "head", None),
            P(None, None, "head"),
        ),
        out_specs=P(("req", "head"), None),
        check_vma=False,
    )
```

profile of v0, /device:TPU:1, one launch (start us, length us, event | category | flops | bytes accessed | tf_op | source)
XLA Modules:
  0.0 306.1 jit_solution(2157831063779013560)
XLA Ops:
  0.0 1.3 dynamic-slice.4
  2.0 0.9 dynamic-update-slice.1
  2.8 0.8 dynamic-update-slice.4
  5.3 20.3 %all-reduce.8 = (s32[256]{0:T(256)S(1)}, s32[256]{0:T(256)S(1)}, s32[256]{0:T(256)S(1)}, s32[256]{0:T(256)S(1)}) all-reduce(s32[256]{0:T(256)S(1)} %dynamic-update-slice.1, s32[256]{0:T(256)S(1)} %dynamic-update-slice.4, s32[256]{0:T(256)S(1)} %dynamic-update-slice.2, s32[256]{0:T(256)S(1)} %dynamic-update-slice.3), channel_id=1, replica_groups=mesh['req'=32,'head'=8] {'req'}, use_global_device_ids=true, to_apply=%add | all-reduce | flops 1024 | bytes 8192
  33.3 1.6 slice_bitcast_fusion
  35.2 35.6 %all_gather.28 = bf16[256,1024]{1,0:T(8,128)(2,1)S(1)} all-gather(bf16[8,1024]{1,0:T(8,128)(2,1)S(1)} %copy-done.2), channel_id=1, replica_groups=mesh['req'=32,'head'=8] {'req'}, dimensions={0}, use_global_device_ids=true | all-gather | bytes 540672 | tf_op jit(solution)/shard_map/all_gather | solution.py:111
  72.4 1.7 fusion.94
  74.6 1.5 fusion.23
  76.7 36.7 %all-reduce.4 = bf16[8,1024]{1,0:T(8,128)(2,1)S(1)} all-reduce(bf16[8,1024]{1,0:T(8,128)(2,1)S(1)} %convolution_convert_fusion.3), channel_id=2, replica_groups=mesh['req'=32,'head'=8] {'head'}, use_global_device_ids=true, to_apply=%region_6.8.clone | all-reduce | flops 8192 | bytes 32768
  114.1 1.3 multiply_reduce_fusion.7
  116.1 16.3 %all-gather = bf16[8,1,1024]{2,1,0:T(2,128)(2,1)S(1)} all-gather(bf16[1,1,1024]{2,1,0:T(2,128)(2,1)S(1)} %convert_bitcast_fusion.2), channel_id=1, replica_groups=mesh['req'=32,'head'=8] {'head'}, dimensions={0}, use_global_device_ids=true | all-gather | bytes 18432 | tf_op jit(solution)/shard_map/all_gather | solution.py:149
  132.4 2.0 fusion.6
  134.3 1.5 convolution_convert_fusion.2
  135.8 20.4 %all-reduce.5 = bf16[8,1024]{1,0:T(8,128)(2,1)S(1)} all-reduce(bf16[8,1024]{1,0:T(8,128)(2,1)S(1)} %convolution_convert_fusion.2), channel_id=3, replica_groups=mesh['req'=32,'head'=8] {'head'}, use_global_device_ids=true, to_apply=%region_8.10.clone | all-reduce | flops 8192 | bytes 32768
  156.2 1.3 multiply_reduce_fusion.6
  158.5 16.3 %all-gather.1 = bf16[8,1,1024]{2,1,0:T(2,128)(2,1)S(1)} all-gather(bf16[1,1,1024]{2,1,0:T(2,128)(2,1)S(1)} %convert_bitcast_fusion.1), channel_id=1, replica_groups=mesh['req'=32,'head'=8] {'head'}, dimensions={0}, use_global_device_ids=true | all-gather | bytes 18432 | tf_op jit(solution)/shard_map/all_gather | solution.py:122
  175.4 1.8 fusion.95
  177.7 1.5 fusion.19
  179.9 20.4 %all-reduce.6 = bf16[8,1024]{1,0:T(8,128)(2,1)S(1)} all-reduce(bf16[8,1024]{1,0:T(8,128)(2,1)S(1)} %convolution_convert_fusion.1), channel_id=4, replica_groups=mesh['req'=32,'head'=8] {'head'}, use_global_device_ids=true, to_apply=%region_14.16.clone | all-reduce | flops 8192 | bytes 32768
  200.3 1.3 multiply_reduce_fusion.5
  202.2 16.3 %all-gather.2 = bf16[8,1,1024]{2,1,0:T(2,128)(2,1)S(1)} all-gather(bf16[1,1,1024]{2,1,0:T(2,128)(2,1)S(1)} %convert_bitcast_fusion), channel_id=1, replica_groups=mesh['req'=32,'head'=8] {'head'}, dimensions={0}, use_global_device_ids=true | all-gather | bytes 18432 | tf_op jit(solution)/shard_map/all_gather | solution.py:149
  218.5 2.0 fusion.9
  220.7 20.4 %all-reduce.7 = bf16[8,1024]{1,0:T(8,128)(2,1)S(1)} all-reduce(bf16[8,1024]{1,0:T(8,128)(2,1)S(1)} %convolution_convert_fusion), channel_id=5, replica_groups=mesh['req'=32,'head'=8] {'head'}, use_global_device_ids=true, to_apply=%region_16.18.clone | all-reduce | flops 8192 | bytes 32768
  241.8 63.7 %all-gather.3 = bf16[256,1,1024]{2,1,0:T(2,128)(2,1)S(1)} all-gather(bf16[1,1,1024]{2,1,0:T(2,128)(2,1)S(1)} %fusion.70), channel_id=1, replica_groups=mesh['req'=32,'head'=8] {'req','head'}, dimensions={0}, use_global_device_ids=true | all-gather | bytes 526336 | tf_op jit(solution)/shard_map/all_gather | solution.py:173
  (86 shorter events, 14.6 us)
Async XLA Ops:
  0.0 71.6 %slice-start = ((f32[2,1024]{1,0:T(2,128)}), f32[1,1024]{1,0:T(1,128)S(1)}, s32[]{:S(2)}) async-start(f32[2,1024]{1,0:T(2,128)} %param.23), calls=%async_computation | async-start | bytes 8192 | tf_op jit(solution)/shard_map/slice | solution.py:120
  0.0 35.2 %copy-start.2 = (bf16[8,1024]{1,0:T(8,128)(2,1)S(1)}, bf16[8,1024]{1,0:T(8,128)(2,1)}, u32[]{:S(2)}) copy-start(bf16[8,1024]{1,0:T(8,128)(2,1)} %param.16) | copy-start | bytes 49156
  33.3 43.3 %copy-start = (bf16[2,128,1024]{2,1,0:T(8,128)(2,1)S(1)}, bf16[2,128,1024]{2,1,0:T(8,128)(2,1)}, u32[]{:S(2)}) copy-start(bf16[2,128,1024]{2,1,0:T(8,128)(2,1)} %param.26) | copy-start | bytes 1572868
  33.3 80.1 %copy-start.5 = (u32[256]{0:T(256)S(1)}, u32[256]{0:T(256)}, u32[]{:S(2)}) copy-start(u32[256]{0:T(256)} %constant.146) | copy-start | bytes 3076
  33.3 82.7 %copy-start.3 = (f32[2,1024]{1,0:T(2,128)S(1)}, f32[2,1024]{1,0:T(2,128)}, u32[]{:S(2)}) copy-start(f32[2,1024]{1,0:T(2,128)} %param.24) | copy-start | bytes 24580
  72.4 86.1 %copy-start.1 = (f32[2,1024]{1,0:T(2,128)S(1)}, f32[2,1024]{1,0:T(2,128)}, u32[]{:S(2)}) copy-start(f32[2,1024]{1,0:T(2,128)} %param.23) | copy-start | bytes 24580
  175.2 45.3 %copy-start.4 = (bf16[2,512,1024]{2,1,0:T(8,128)(2,1)S(1)}, bf16[2,512,1024]{2,1,0:T(8,128)(2,1)}, u32[]{:S(2)}) copy-start(bf16[2,512,1024]{2,1,0:T(8,128)(2,1)} %param.28) | copy-start | bytes 6291460
where the time goes:
time: 307 us; the launch traced here: 306 us
  blocking collectives  266 us (87%)
  matrix products  13.4 us (4%)
  local copies, waits for them, and re-layouts  11.9 us (4%)
  other arithmetic  9.74 us (3%)
  between operations  4.82 us (2%)
    unnamed x5, blocking collectives  118 us
    all_gather x1, blocking collectives, per_device(): everything = lax.all_gather(final_rows, ('req', 'head'), axis=0, tiled=True)  63.7 us
    all_gather x1, blocking collectives, per_device(): all_tokens = lax.all_gather(tokens, 'req', axis=0, tiled=True)  35.6 us
    all_gather x2, blocking collectives, per_device(): lax.all_gather(rms_scale(residual, ffn_gain[layer_index]).astype(jnp.bflo...  32.6 us
    all_gather x1, blocking collectives, per_device(): lax.all_gather(rms_scale(residual, attn_gain[layer_index]).astype(jnp.bfl...  16.3 us

commit v1 on v0

v1 whole, which is shorter than its diff:
```python
import functools

import jax
import jax.numpy as jnp
import numpy as np
from jax import lax
from jax.experimental import pallas as pl
from jax.experimental.pallas import tpu as pltpu
from jax.sharding import PartitionSpec as P

HD = 64
LAYERS = 2
LANES = 128
NEG = -1e30
MESH = pl.DeviceIdType.MESH
F32, BF16, I32 = jnp.float32, jnp.bfloat16, jnp.int32


def ring_order(count):
    return sorted(range(count), key=lambda d: -min(d, count - d))


def req_order(y_count, z_count):
    pairs = [(dy, dz) for dy in range(y_count) for dz in range(z_count) if dy or dz]
    return sorted(pairs, key=lambda p: -(min(p[0], y_count - p[0]) + min(p[1], z_count - p[1])))


def head_order(count):
    return sorted(range(1, count), key=lambda d: -min(d // 2, (count - d) // 2))


def iota(shape, axis):
    return lax.broadcasted_iota(I32, shape, axis)


def column(scalars, shape):
    rows = iota(shape, 0) % 8
    out = jnp.zeros(shape, I32)
    for i, s in enumerate(scalars):
        out = jnp.where(rows == i, s, out)
    return out


def rms(stream, gain):
    return stream * lax.rsqrt(jnp.mean(stream * stream, axis=-1, keepdims=True) + 1e-06) * gain


def angles(times, freq):
    lane = iota((8, LANES), 1)
    theta = times.astype(F32) * freq
    sine = jnp.sin(theta)
    return jnp.cos(theta), jnp.where(lane % HD < HD // 2, -sine, sine)


def rotate(u, cosine, sine):
    lane = iota((8, LANES), 1)
    partner = jnp.where(lane % HD < HD // 2, pltpu.roll(u, LANES - HD // 2, 1), pltpu.roll(u, HD // 2, 1))
    return u * cosine + partner * sine


def split_qkv(proj, cosine, sine):
    low = iota((8, LANES), 1) < HD
    t0, t1, t2 = proj[:, :128], proj[:, 128:256], proj[:, 256:384]
    q = jnp.where(low, t0, t1)
    k = pltpu.roll(jnp.where(low, t2, t0), HD, 1)
    v = jnp.where(low, t1, t2)
    q = rotate(q, cosine, sine).astype(BF16)
    k = rotate(k, cosine, sine).astype(BF16)
    prod = q.astype(F32) * k.astype(F32)
    s0 = jnp.sum(jnp.where(low, prod, 0.0), axis=1, keepdims=True) * (HD ** -0.5)
    s1 = jnp.sum(jnp.where(low, 0.0, prod), axis=1, keepdims=True) * (HD ** -0.5)
    return q, v.astype(BF16), s0, s1


def kernel(
    nr, nh, ny, nz,
    tok_h, len_h, own_h, pos_h, var_h, cv_h, kv_h, ag_h, fg_h, qkv_h, out_h, gu_h, dn_h, vb_h, fr_h,
    o_ref,
    tok, cv, kv, ag, fg, qkv, outw, gu, dn, vb, freq,
    len_s, own_s, pos_s, var_s,
    qv_send, meta_send, qv_recv, meta_recv, tok_recv, ar, last_send, last_recv,
    load_sem, send1, recv1, sendm, recvm, sendt, recvt, ar_send, ar_recv, send2, recv2,
):
    me_r = lax.axis_index("req")
    me_h = lax.axis_index("head")
    y, z = me_r // nz, me_r % nz
    peers_r = [(((y + dy) % ny) * nz + (z + dz) % nz) for dy, dz in req_order(ny, nz)]
    peers_h = [(me_h + d) % nh for d in head_order(nh)]

    barrier = pltpu.get_barrier_semaphore()
    for r in peers_r:
        pl.semaphore_signal(barrier, inc=1, device_id=(r, me_h), device_id_type=MESH)
    for h in peers_h:
        pl.semaphore_signal(barrier, inc=1, device_id=(me_r, h), device_id_type=MESH)

    loads = []

    def load(src, dst):
        copy = pltpu.make_async_copy(src, dst, load_sem.at[len(loads)])
        copy.start()
        loads.append(copy)
        return copy

    first = [load(tok_h, tok), load(ag_h, ag), load(pos_h, pos_s), load(len_h, len_s), load(var_h, var_s)]
    first.append(load(fr_h, freq))
    first += [load(qkv_h.at[0], qkv.at[0]), load(own_h, own_s)]
    att_in = [[load(vb_h, vb), load(cv_h, cv), load(kv_h.at[0, 0], kv.at[0, 0])]]
    val_in = [[load(kv_h.at[0, 1], kv.at[0, 1])]]
    out_in = [[load(out_h.at[0], outw.at[0])]]
    gu_in = [[load(fg_h, fg), load(gu_h.at[0], gu.at[0])]]
    dn_in = [[load(dn_h.at[0], dn.at[0])]]
    qkv_in = [[], [load(qkv_h.at[1], qkv.at[1])]]
    att_in.append([load(kv_h.at[1, 0], kv.at[1, 0])])
    val_in.append([load(kv_h.at[1, 1], kv.at[1, 1])])
    out_in.append([load(out_h.at[1], outw.at[1])])
    gu_in.append([load(gu_h.at[1], gu.at[1])])
    dn_in.append([load(dn_h.at[1], dn.at[1])])

    def arrive(copies):
        for c in copies:
            c.wait()

    arrive(first)
    lane8 = iota((8, LANES), 1)
    row8 = iota((8, LANES), 0)
    cosine, sine = angles(column([pos_s[i] for i in range(8)], (8, LANES)), freq[...])
    normed = rms(tok[...].astype(F32), ag[0:1, :]).astype(BF16)
    proj = jnp.dot(normed, qkv[0], preferred_element_type=F32)
    q, v, s0, s1 = split_qkv(proj, cosine, sine)
    qv = jnp.concatenate([q, v], axis=0)
    kind = lane8 % 16
    meta = jnp.where(kind == 0, column([len_s[i] for i in range(8)], (8, LANES)).astype(F32), 0.0)
    meta = jnp.where(kind == 1, column([var_s[i] for i in range(8)], (8, LANES)).astype(F32), meta)
    meta = jnp.where(kind == 2, column([pos_s[i] for i in range(8)], (8, LANES)).astype(F32), meta)
    meta = jnp.where(kind == 3, s0, meta)
    meta = jnp.where(kind == 4, s1, meta)
    meta = jnp.sum(jnp.where(lane8 // 16 == row8, meta, 0.0), axis=0, keepdims=True)
    my_cols = pl.ds(pl.multiple_of(me_h * LANES, LANES), LANES)
    qv_send[...] = qv
    meta_send[...] = meta
    qv_recv[me_r] = qv
    meta_recv[me_r] = meta
    tok_recv[me_r] = tok[:, my_cols]

    pl.semaphore_wait(barrier, len(peers_r) + len(peers_h))

    def send(src, dst, s, r, to):
        pltpu.make_async_remote_copy(
            src_ref=src, dst_ref=dst, send_sem=s, recv_sem=r, device_id=to, device_id_type=MESH
        ).start()

    def finish(ref, sem):
        pltpu.make_async_copy(ref, ref, sem).wait()

    for r in peers_r:
        send(qv_send, qv_recv.at[me_r], send1, recv1, (r, me_h))
        send(meta_send, meta_recv.at[me_r], sendm, recvm, (r, me_h))
    for r in peers_r:
        send(tok.at[:, my_cols], tok_recv.at[me_r], sendt, recvt, (r, me_h))

    owners = [own_s[i] for i in range(8)]
    bases = [(o // 8) * 16 + o % 8 for o in owners]
    pick = column(bases, (16, nr * 16)) + jnp.where(iota((16, nr * 16), 0) >= 8, 8, 0)
    pick = jnp.where(iota((16, nr * 16), 1) == pick, 1.0, 0.0).astype(BF16)
    row16 = iota((16, LANES), 0)
    lane16 = iota((16, LANES), 1)
    half16 = (lane16 // HD) == (row16 // 8)
    low8 = lane8 < HD

    others = pl.ds(0, nr - 1)
    arrive(att_in[0])
    finish(qv_recv.at[others], recv1)
    picked = jnp.dot(pick, qv_recv[...].reshape(nr * 16, LANES), preferred_element_type=F32)
    q, v = picked[:8], picked[8:]
    finish(meta_recv.at[others], recvm)
    meta = jnp.zeros((8, LANES), F32)
    for t, o in enumerate(owners):
        meta = jnp.where(row8 == t, meta_recv[o // 8], meta)
    mine = lane8 // 16 == column([o % 8 for o in owners], (8, LANES))
    meta = [
        jnp.sum(jnp.where(mine & (kind == i), meta, 0.0), axis=1, keepdims=True) for i in range(5)
    ]
    length, variate, time = meta[0].astype(I32), meta[1].astype(I32), meta[2]
    s0, s1 = meta[3], meta[4]
    same_var = cv[...] == variate
    live = iota((8, 512), 1) < length
    live = jnp.concatenate([live.astype(F32)] * 2, axis=0) > 0.5

    def attend(layer, q, v, s0, s1):
        q2 = jnp.where(half16, jnp.concatenate([q, q], axis=0), 0.0)
        raw = jnp.zeros((16, 512), F32)
        for p in range(4):
            qp = jnp.concatenate(
                [jnp.where(row16 % 8 == 2 * p + i, q2, 0.0) for i in range(2)], axis=1
            ).astype(BF16)
            kp = jnp.concatenate([kv[layer, 0, 2 * p], kv[layer, 0, 2 * p + 1]], axis=1)
            raw += lax.dot_general(qp, kp, (((1,), (1,)), ((), ())), preferred_element_type=F32)
        table = vb[layer]
        bias = jnp.concatenate(
            [jnp.where(same_var, table[0:1, h : h + 1], table[1:2, h : h + 1]) for h in range(2)], axis=0
        )
        scores = jnp.where(live, raw * (HD ** -0.5) + bias, NEG)
        own = jnp.concatenate([s0 + table[0:1, 0:1], s1 + table[0:1, 1:2]], axis=0)
        top = jnp.maximum(jnp.max(scores, axis=1, keepdims=True), own)
        weights = jnp.exp(scores - top)
        own_weight = jnp.exp(own - top)
        total = jnp.sum(weights, axis=1, keepdims=True) + own_weight
        probs = (weights / total).astype(BF16)
        own_prob = (own_weight / total).astype(BF16).astype(F32)
        arrive(val_in[layer])
        mixed = jnp.zeros((16, LANES), F32)
        for p in range(4):
            vp = jnp.concatenate([kv[layer, 1, 2 * p], kv[layer, 1, 2 * p + 1]], axis=1)
            got = jnp.dot(probs, vp, preferred_element_type=F32)
            mixed = jnp.where(row16 % 8 == 2 * p, got[:, :128], mixed)
            mixed = jnp.where(row16 % 8 == 2 * p + 1, got[:, 128:], mixed)
        mixed = mixed + own_prob * jnp.concatenate([v, v], axis=0)
        att = jnp.where(low8, mixed[:8], mixed[8:]).astype(BF16)
        arrive(out_in[layer])
        return jnp.dot(att, outw[layer], preferred_element_type=F32)

    def reduce(step, partial):
        folded = jnp.concatenate([partial[:, :512], partial[:, 512:]], axis=0).astype(BF16)
        ar[step, me_h] = folded
        for h in peers_h:
            send(ar.at[step, me_h], ar.at[step, me_h], ar_send.at[step], ar_recv.at[step], (me_r, h))
        return lambda: collect(step)

    def collect(step):
        finish(ar.at[step, pl.ds(0, nh - 1)], ar_recv.at[step])
        total = jnp.sum(ar[step].astype(F32), axis=0)
        return jnp.concatenate([total[:8], total[8:]], axis=1)

    def feed_forward(layer, stream):
        arrive(gu_in[layer])
        normed = rms(stream, fg[layer : layer + 1, :]).astype(BF16)
        gate = jnp.dot(normed, gu[layer, 0], preferred_element_type=F32)
        up = jnp.dot(normed, gu[layer, 1], preferred_element_type=F32)
        hidden = (gate / (1.0 + jnp.exp(-gate)) * up).astype(BF16)
        arrive(dn_in[layer])
        return jnp.dot(hidden, dn[layer], preferred_element_type=F32)

    partial = attend(0, q, v, s0, s1)
    finish(tok_recv.at[others], recvt)
    pick_row = iota((8, nr * 8), 1) == column(owners, (8, nr * 8))
    rows = jnp.dot(
        jnp.where(pick_row, 1.0, 0.0).astype(BF16),
        tok_recv[...].reshape(nr * 8, LANES),
        preferred_element_type=F32,
    )
    partial = partial + jnp.where(
        iota(partial.shape, 1) // LANES == me_h, jnp.concatenate([rows] * (partial.shape[1] // LANES), axis=1), 0.0
    )
    done = reduce(0, partial)
    cosine, sine = angles(jnp.broadcast_to(time, (8, LANES)), freq[...])
    stream = done()
    done = reduce(1, feed_forward(0, stream))
    stream = stream + done()

    arrive(qkv_in[1])
    normed = rms(stream, ag[1:2, :]).astype(BF16)
    q, v, s0, s1 = split_qkv(jnp.dot(normed, qkv[1], preferred_element_type=F32), cosine, sine)
    arrive(att_in[1])
    done = reduce(2, attend(1, q.astype(F32), v.astype(F32), s0, s1))
    stream = stream + done()
    done = reduce(3, feed_forward(1, stream))
    owner_lane = jnp.zeros((nr * 8, 64), I32)
    lane64 = iota((nr * 8, 64), 1)
    for t, o in enumerate(owners):
        owner_lane = jnp.where(lane64 % 8 == t, o, owner_lane)
    row_r = iota((nr * 8, 64), 0)
    route = (row_r % 8 == lane64 // 8) & (owner_lane == (row_r // 8) * nh + me_h)
    route = jnp.where(route, 1.0, 0.0).astype(BF16)
    stream = stream + done()
    final = jnp.concatenate([stream[:, c * LANES : (c + 1) * LANES] for c in range(8)], axis=0).astype(BF16)
    routed = jnp.dot(route, final, preferred_element_type=F32)
    last_send[...] = routed.reshape(nr, 8, LANES).astype(BF16)
    for r in peers_r:
        send(last_send.at[r], last_recv.at[me_r], send2, recv2, (r, me_h))
    last_recv[me_r] = last_send[me_r]
    for ref, sem in (
        (qv_recv.at[others], send1),
        (meta_recv.at[others], sendm),
        (tok_recv.at[others], sendt),
        *((ar.at[i, pl.ds(0, nh - 1)], ar_send.at[i]) for i in range(4)),
        (last_recv.at[others], send2),
    ):
        finish(ref, sem)
    finish(last_recv.at[others], recv2)
    row = jnp.sum(last_recv[...].astype(F32), axis=0)
    for c in range(8):
        o_ref[:, c * LANES : (c + 1) * LANES] = row[c : c + 1, :].astype(BF16)


def solution(mesh):
    nr, nh = mesh.shape["req"], mesh.shape["head"]
    nz = min(8, nr)
    ny = nr // nz

    def per_device(*args):
        d = args[0].shape[1]
        vmem = lambda a: pltpu.VMEM(a.shape, a.dtype)
        freq = jnp.asarray(10000.0 ** (-2.0 * (np.arange(LANES)[None] % (HD // 2)) / HD), F32)
        args = (*args, freq)
        tok, lengths, owner, positions, variates, cv, kv, ag, fg, qkv, outw, gu, dn, vb, _ = args
        dma = pltpu.SemaphoreType.DMA
        return pl.pallas_call(
            functools.partial(kernel, nr, nh, ny, nz),
            out_shape=jax.ShapeDtypeStruct((1, d), BF16),
            in_specs=[pl.BlockSpec(memory_space=pl.ANY)] * len(args),
            out_specs=pl.BlockSpec(memory_space=pltpu.VMEM),
            scratch_shapes=[vmem(a) for a in (tok, cv, kv, ag, fg, qkv, outw, gu, dn, vb, freq)]
            + [pltpu.SMEM(a.shape, a.dtype) for a in (lengths, owner, positions, variates)]
            + [
                pltpu.VMEM((16, LANES), BF16),
                pltpu.VMEM((1, LANES), F32),
                pltpu.VMEM((nr, 16, LANES), BF16),
                pltpu.VMEM((nr, 1, LANES), F32),
                pltpu.VMEM((nr, 8, LANES), BF16),
                pltpu.VMEM((4, nh, 16, 512), BF16),
                pltpu.VMEM((nr, 8, LANES), BF16),
                pltpu.VMEM((nr, 8, LANES), BF16),
                dma((22,)),
                dma, dma, dma, dma, dma, dma,
                dma((4,)),
                dma((4,)),
                dma, dma,
            ],
            compiler_params=pltpu.CompilerParams(collective_id=0, has_side_effects=True),
            name="decode",
        )(*args)

    return jax.shard_map(
        per_device,
        mesh=mesh,
        in_specs=(
            P("req", None),
            P("req"),
            P("req"),
            P("req"),
            P("req"),
            P("req", None),
            P(None, None, "req", None, "head"),
            P(),
            P(),
            P(None, None, "head"),
            P(None, "head", None),
            P(None, None, None, "head"),
            P(None, "head", None),
            P(None, None, "head"),
        ),
        out_specs=P(("req", "head"), None),
        check_vma=False,
    )
```

time: 307 us -> 46.3 us (0.15)
  blocking collectives: 266 us -> 0 us
  Pallas kernels: 0 us -> 44.8 us
  matrix products: 13.4 us -> 0 us
  local copies, waits for them, and re-layouts: 11.9 us -> 1.28 us
  other arithmetic: 9.74 us -> 0 us
  between operations: 4.82 us -> 0.01 us
    all_gather x5 -> x0, blocking collectives: 148 us -> none  [the longest x1 63.7 us: per_device(): everything = lax.all_gather(final_rows, ('req', 'head'), axis=0, tiled=True)]
    unnamed x5 -> x0, blocking collectives: 118 us -> none
    pallas_call x0 -> x1, Pallas kernels: none -> 44.8 us  [per_device(): pl.pallas_call(functools.partial(kernel, nr, nh, ny, nz), out_shape=jax.S...]
    dot_general x12 -> x0, matrix products: 13.4 us -> none  [the longest x2 3.92 us: per_device(): jnp.einsum('rd,gdf->grf', ffn_input, gate_up_weight[layer_index], preferr...]
    reduce_sum x11 -> x0, other arithmetic: 5.55 us -> none  [the longest x4 4.04 us: rms_scale(): jnp.mean(stream * stream, axis=-1, keepdims=True) + 1e-06]
    unnamed x22 -> x1, local copies, waits for them, and re-layouts: 5.27 us -> 1.28 us
where the time goes in v1:
time: 46.3 us; the launch traced here: 46.1 us
  Pallas kernels  44.8 us (97%)
  local copies, waits for them, and re-layouts  1.28 us (3%)
    pallas_call x1, Pallas kernels, per_device(): pl.pallas_call(functools.partial(kernel, nr, nh, ny, nz), out_shape=jax.S...  44.8 us
    unnamed x1, local copies, waits for them, and re-layouts  1.28 us

profile of v1, /device:TPU:1, one launch (start us, length us, event | category | flops | bytes accessed | tf_op | source)
XLA Modules:
  0.0 46.1 jit_solution(12852163171533071502)
XLA Ops:
  0.0 44.8 %decode.1 = bf16[1,1024]{1,0:T(2,128)(2,1)} custom-call(bf16[8,1024]{1,0:T(8,128)(2,1)} %tok_h.1, s32[8]{0:T(128)} %len_h.1, s32[8]{0:T(128)} %own_h.1, s32[8]{0:T(128)} %pos_h.1, s32[8]{0:T(128)} %var_h.1, s32[8,512]{1,0:T(8,128)} %cv_h.1, bf16[2,2,8,512,128]{4,3,2,1,0:T(8,128)(2,1)} %kv_h.1, f32[2,1024]{1,0:T(2,128)} %ag_h.1, f32[2,1024]{1,0:T(2,128)} %fg_h.1, ...), custom_call_target="tpu_custom_call" | custom-call | tf_op jit(solution)/shard_map/decode/pallas_call | solution.py:307
  44.8 1.3 %copy.17 = bf16[1,1024]{1,0:T(2,128)(2,1)} copy(bf16[1,1024]{1,0:T(2,128)(2,1)} %decode.1) | data formatting | bytes 4096
